TPU v7x, 256 devices: a whole 4x4x8 slice. The times are simulated.
256 devices in a mesh: wide: 32 (over x, y, core), narrow: 8 (over z).
Axes of the slice: x: 4, y: 4, z: 8, core: 2. Of those that a mesh axis runs over, the one named last changes fastest.
Arguments:
- gradient: float32 [2, 8192, 2048], P(None, 'wide', 'narrow'), may hold values from -6 to 6
- probe_modes: bfloat16 [4, 2, 256, 256], replicated, may hold values from -5 to 5
- mode_weights: bfloat16 [32, 8, 3, 4, 2, 256, 256], P('wide', 'narrow'), may hold values from -4 to 4
- offsets: int32 [32, 8, 3, 2], P('wide', 'narrow'), may hold values from -64 to 64, as said below
- counts: int32 [32, 8], P('wide', 'narrow'), may hold values from 1 to 3, as said below
Outputs:
- solution: float32 [2, 8192, 2048], P(None, 'wide', 'narrow')
- residual: float32 [2, 8192, 2048], P(None, 'wide', 'narrow')
Inputs may be any that keep to these rules, and one draw needn't show every extreme that they name: `offsets`: each offset lies between -64 and 64; both ends are taken by some slot in every draw. `counts`: slots from a tile's count on are empty; some tile has all 3 slots live in every draw.
All inputs are finite; a program needn't handle non-finite values.
Results may differ from a plain program's by a relative error of at most 0.012.
Values sent between devices are 32-bit elements; how exact they have to be, the bound alone decides.
A program may use at most 128 MiB of HBM per device.

v0:
```python
import functools
import math

import jax
import jax.numpy as jnp
from jax import lax
from jax.sharding import Mesh
from jax.sharding import PartitionSpec as P

W = 256
STEPS = 2
HALO = 64
WIDE = ("wide_0", "wide_1", "wide_2")
WIDE_NARROW = ("wide_0", "wide_1", "wide_2", "narrow")


damping = 0.5


def padded(x, sides, width):
    for axis, dim in sides:
        peers, length = (lax.axis_size(axis), x.shape[dim])
        up = [(i, (i + 1) % peers) for i in range(peers - 1)]
        down = [(j, i) for i, j in up]
        last = lax.slice_in_dim(x, length - width, length, axis=dim)
        initial = lax.slice_in_dim(x, 0, width, axis=dim)
        before = lax.ppermute(last, axis, up)
        after = lax.ppermute(initial, axis, down)
        x = jnp.concatenate([before, x, after], axis=dim)
    return x


def one_axis_at_a_time(x, axes):
    return functools.reduce(lax.psum, axes, x)


def dft_tables(length, sign):
    counter = jnp.arange(length, dtype=jnp.int32)
    phases = counter[:, None] * counter[None, :] % length
    angles = phases.astype(jnp.float32) * (2.0 * math.pi / length)
    factor = 1.0 / math.sqrt(length)
    real_part = jnp.cos(angles) * factor
    imag_part = -sign * jnp.sin(angles) * factor
    left_table = jnp.stack(
        [jnp.stack([real_part, -imag_part]), jnp.stack([imag_part, real_part])]
    ).astype(jnp.bfloat16)
    right_table = jnp.stack(
        [jnp.stack([real_part, imag_part]), jnp.stack([-imag_part, real_part])]
    ).astype(jnp.bfloat16)
    return (left_table, right_table)


def left_apply(table, values):
    return jnp.einsum("pqab,nqbc->npac", table, values, preferred_element_type=jnp.float32)


def right_apply(table, values):
    return jnp.einsum("nqac,qpcd->npad", values, table, preferred_element_type=jnp.float32)


def wave_pass(patches, probe_modes, weights, live_mask, forward_tables, inverse_tables):
    frames = patches.shape[0]
    modes = probe_modes.shape[0]
    length = probe_modes.shape[-1]
    probe_re = probe_modes[None, :, 0].astype(jnp.float32)
    probe_im = probe_modes[None, :, 1].astype(jnp.float32)
    patch_re = patches[:, None, 0]
    patch_im = patches[:, None, 1]
    exit_wave = jnp.stack(
        [probe_re * patch_re - probe_im * patch_im, probe_re * patch_im + probe_im * patch_re],
        axis=2,
    ).astype(jnp.bfloat16)
    stacked = exit_wave.reshape(frames * modes, 2, length, length)
    partial_value = left_apply(forward_tables[0], stacked).astype(jnp.bfloat16)
    far_field = right_apply(forward_tables[1], partial_value).reshape(
        frames, modes, 2, length, length
    )
    weight_re = weights[:, :, 0].astype(jnp.float32)
    weight_im = weights[:, :, 1].astype(jnp.float32)
    projected = (
        jnp.sum(weight_re * far_field[:, :, 0] + weight_im * far_field[:, :, 1], axis=1)
        * live_mask[:, None, None]
    )
    weighted = jnp.stack(
        [weight_re * projected[:, None], weight_im * projected[:, None]], axis=2
    ).astype(jnp.bfloat16)
    partial_back = left_apply(
        inverse_tables[0], weighted.reshape(frames * modes, 2, length, length)
    ).astype(jnp.bfloat16)
    near_field = right_apply(inverse_tables[1], partial_back).reshape(
        frames, modes, 2, length, length
    )
    near_re = near_field[:, :, 0]
    near_im = near_field[:, :, 1]
    contribution = jnp.stack(
        [
            jnp.sum(probe_re * near_re + probe_im * near_im, axis=1),
            jnp.sum(probe_re * near_im - probe_im * near_re, axis=1),
        ],
        axis=1,
    )
    return (contribution, projected)


def fold_margins(total):
    length = total.shape[1] - 2 * HALO
    inner_gap = length - 2 * HALO
    extent = total.shape[2]
    row_strips = jnp.concatenate(
        [
            total[:, :HALO],
            jnp.zeros((2, inner_gap, extent), jnp.float32),
            total[:, HALO + length :],
        ],
        axis=1,
    )
    arrived_rows = padded(row_strips, ((WIDE, 1),), HALO)
    middle = total[:, HALO : HALO + length]
    middle = middle.at[:, :HALO].add(arrived_rows[:, :HALO])
    middle = middle.at[:, length - HALO :].add(arrived_rows[:, HALO + length :])
    col_strips = jnp.concatenate(
        [
            middle[:, :, :HALO],
            jnp.zeros((2, length, inner_gap), jnp.float32),
            middle[:, :, HALO + length :],
        ],
        axis=2,
    )
    arrived_cols = padded(col_strips, (("narrow", 2),), HALO)
    inner = middle[:, :, HALO : HALO + length]
    inner = inner.at[:, :, :HALO].add(arrived_cols[:, :, :HALO])
    inner = inner.at[:, :, length - HALO :].add(arrived_cols[:, :, HALO + length :])
    return inner


def apply_operator(
    direction, probe_modes, mode_weights, offsets, counts, forward_tables, inverse_tables
):
    extended = padded(direction, ((WIDE, 1), ("narrow", 2)), HALO)
    total = jnp.zeros_like(extended)

    def visit(slot_index, carried):
        running, squares = carried
        row_start = HALO + offsets[0, 0, slot_index, 0]
        col_start = HALO + offsets[0, 0, slot_index, 1]
        patch = lax.dynamic_slice(extended, (0, row_start, col_start), (2, W, W))
        frame_weights = lax.dynamic_index_in_dim(mode_weights[0, 0], slot_index, 0, keepdims=True)
        contribution, projected = wave_pass(
            patch[None],
            probe_modes,
            frame_weights,
            jnp.ones((1,), jnp.float32),
            forward_tables,
            inverse_tables,
        )
        region = lax.dynamic_slice(running, (0, row_start, col_start), (2, W, W))
        running = lax.dynamic_update_slice(
            running, region + contribution[0], (0, row_start, col_start)
        )
        return (running, squares + jnp.sum(projected * projected))

    total, squares = lax.fori_loop(0, counts[0, 0], visit, (total, jnp.float32(0.0)))
    return (fold_margins(total) + damping * direction, squares)


def global_sum(value):
    return one_axis_at_a_time(value, WIDE_NARROW)


def local(gradient, probe_modes, mode_weights, offsets, counts):
    forward_tables = dft_tables(W, 1.0)
    inverse_tables = dft_tables(W, -1.0)
    solution = jnp.zeros_like(gradient)
    residual = gradient
    direction = gradient
    norm_now = global_sum(jnp.sum(residual * residual))
    for iteration in range(STEPS):
        image, squares = apply_operator(
            direction, probe_modes, mode_weights, offsets, counts, forward_tables, inverse_tables
        )
        curvature = global_sum(jnp.sum(direction * image))
        alpha = norm_now / curvature
        solution = solution + alpha * direction
        residual = residual - alpha * image
        if iteration + 1 < STEPS:
            norm_next = global_sum(jnp.sum(residual * residual))
            direction = residual + norm_next / norm_now * direction
            norm_now = norm_next
    return (solution, residual)


def solution(mesh):
    torus = Mesh(
        mesh.devices.reshape(4, 4, 2, mesh.shape["narrow"]),
        ("wide_0", "wide_1", "wide_2", "narrow"),
    )
    placed = (
        P(None, WIDE, "narrow"),
        P(),
        P(WIDE, "narrow", None, None, None, None, None),
        P(WIDE, "narrow", None, None),
        P(WIDE, "narrow"),
    )
    return jax.shard_map(
        local,
        mesh=torus,
        in_specs=placed,
        out_specs=(P(None, WIDE, "narrow"), P(None, WIDE, "narrow")),
        check_vma=False,
    )
```

profile of v0, /device:TPU:1, one launch (start us, length us, event | category | flops | bytes accessed | tf_op | source)
XLA Modules:
  0.0 384.2 jit_solution(12757233228075539911)
XLA Ops:
  1.6 4.6 %collective-permute-start = (f32[2,64,256]{2,1,0:T(8,128)S(1)}, f32[2,64,256]{2,1,0:T(8,128)S(1)}, u32[]{:S(2)}, u32[]{:S(2)}) collective-permute-start(f32[2,64,256]{2,1,0:T(8,128)S(1)} %get-tuple-element.603), channel_id=1, source_target_pairs={{0,8},{8,16},{16,24},{24,32},{32,40},{40,48},{48,56},{56,64},{64,7... | collective-permute-start | bytes 393224 | tf_op jit(solution)/shard_map/ppermute | solution.py:27
  25.4 4.4 %collective-permute-done.2 = f32[2,384,64]{2,1,0:T(8,128)S(1)} collective-permute-done((f32[2,384,64]{2,1,0:T(8,128)S(1)}, f32[2,384,64]{2,1,0:T(8,128)S(1)}, u32[]{:S(2)}, u32[]{:S(2)}) %collective-permute-start.2) | collective-permute-done | bytes 196640 | tf_op jit(solution)/shard_map/ppermute | solution.py:27
  36.5 47.8 %while.38 = (s32[]{:T(128)}, f32[2,384,384]{2,1,0:T(8,128)}, s32[]{:T(128)}, s32[1,1,3,2]{2,3,1,0:T(2,128)S(1)}, bf16[4,2,256,256]{3,2,0,1:T(8,128)(2,1)S(1)}, /...) while((s32[]{:T(128)}, f32[2,384,384]{2,1,0:T(8,128)}, ...), condition=%wide.region_9.10_spmd, body=%wide.region_5.9_spmd.sunk | while | flops 2158034944 | bytes 27525440 | solution.py:162
  53.8 6.3 %dynamic_update_slice.18 = f32[2,384,384]{2,1,0:T(8,128)} dynamic-update-slice(f32[2,384,384]{2,1,0:T(8,128)} %get-tuple-element.805, f32[2,256,256]{2,1,0:T(8,128)S(1)} %fusion.124, s32[]{:T(128)} %constant.314.clone.1..sunk, s32[]{:T(128)S(6)} %select_n.148, s32[]{:T(128)S(6)} %select_n.149) | dynamic-update-slice | bytes 1048580 | tf_op jit(solution)/shard_map/while/body/dynamic_update_slice | solution.py:157
  77.4 6.2 %dynamic_update_slice.18 = f32[2,384,384]{2,1,0:T(8,128)} dynamic-update-slice(f32[2,384,384]{2,1,0:T(8,128)} %get-tuple-element.805, f32[2,256,256]{2,1,0:T(8,128)S(1)} %fusion.124, s32[]{:T(128)} %constant.314.clone.1..sunk, s32[]{:T(128)S(6)} %select_n.148, s32[]{:T(128)S(6)} %select_n.149) | dynamic-update-slice | bytes 1048580 | tf_op jit(solution)/shard_map/while/body/dynamic_update_slice | solution.py:157
  95.6 26.7 %collective-permute-start.6 = (f32[2,256,64]{2,1,0:T(8,128)S(1)}, f32[2,256,64]{2,1,0:T(8,128)S(1)}, u32[]{:S(2)}, u32[]{:S(2)}) collective-permute-start(f32[2,256,64]{2,1,0:T(8,128)S(1)} %get-tuple-element.597), channel_id=1, source_target_pairs={{0,1},{1,2},{2,3},{3,4},{4,5},{5,6},{6,7},{8,9},{9,10},{10,11},{11... | collective-permute-start | bytes 393224 | tf_op jit(solution)/shard_map/ppermute | solution.py:27
  132.4 16.1 %all-reduce.2 = (f32[]{:T(128)}, f32[]{:T(128)}) all-reduce(f32[]{:T(128)} %get-tuple-element.521, f32[]{:T(128)} %get-tuple-element.520), channel_id=1, replica_groups=mesh['wide_0'=4,'wide_1'=4,'wide_2'=2,'narrow'=8] {'wide_0'}, use_global_device_ids=true, to_apply=%region_1.2 | all-reduce | flops 2 | bytes 16 | tf_op jit(solution)/shard_map/psum | solution.py:34
  148.5 7.5 %all-reduce.1 = (f32[]{:T(128)}, f32[]{:T(128)}) all-reduce(f32[]{:T(128)} %get-tuple-element.570, f32[]{:T(128)} %get-tuple-element.571), channel_id=1, replica_groups=mesh['wide_0'=4,'wide_1'=4,'wide_2'=2,'narrow'=8] {'wide_1'}, use_global_device_ids=true, to_apply=%region_2.3 | all-reduce | flops 2 | bytes 16 | tf_op jit(solution)/shard_map/psum | solution.py:34
  156.1 6.8 %all-reduce.3 = (f32[]{:T(128)}, f32[]{:T(128)}) all-reduce(f32[]{:T(128)} %get-tuple-element.568, f32[]{:T(128)} %get-tuple-element.569), channel_id=1, replica_groups=mesh['wide_0'=4,'wide_1'=4,'wide_2'=2,'narrow'=8] {'wide_2'}, use_global_device_ids=true, to_apply=%region_3.4 | all-reduce | flops 2 | bytes 16 | tf_op jit(solution)/shard_map/psum | solution.py:34
  162.8 13.2 %all-reduce = (f32[]{:T(128)}, f32[]{:T(128)}) all-reduce(f32[]{:T(128)} %get-tuple-element.572, f32[]{:T(128)} %get-tuple-element.573), channel_id=1, replica_groups=mesh['wide_0'=4,'wide_1'=4,'wide_2'=2,'narrow'=8] {'narrow'}, use_global_device_ids=true, to_apply=%region_4.5 | all-reduce | flops 2 | bytes 16 | tf_op jit(solution)/shard_map/psum | solution.py:34
  178.1 8.1 %psum.120 = f32[]{:T(128)} all-reduce(f32[]{:T(128)} %multiply_reduce_fusion.1), channel_id=1, replica_groups=mesh['wide_0'=4,'wide_1'=4,'wide_2'=2,'narrow'=8] {'wide_0'}, use_global_device_ids=true, to_apply=%region_16.17 | all-reduce | flops 1 | bytes 8 | tf_op jit(solution)/shard_map/psum | solution.py:34
  186.1 7.5 %psum.121 = f32[]{:T(128)} all-reduce(f32[]{:T(128)} %psum.120), channel_id=1, replica_groups=mesh['wide_0'=4,'wide_1'=4,'wide_2'=2,'narrow'=8] {'wide_1'}, use_global_device_ids=true, to_apply=%region_17.18 | all-reduce | flops 1 | bytes 8 | tf_op jit(solution)/shard_map/psum | solution.py:34
  193.6 10.7 %psum.122 = f32[]{:T(128)} all-reduce(f32[]{:T(128)} %psum.121), channel_id=1, replica_groups=mesh['wide_0'=4,'wide_1'=4,'wide_2'=2,'narrow'=8] {'wide_2'}, use_global_device_ids=true, to_apply=%region_18.19 | all-reduce | flops 1 | bytes 8 | tf_op jit(solution)/shard_map/psum | solution.py:34
  204.4 11.7 %psum.123 = f32[]{:T(128)} all-reduce(f32[]{:T(128)} %psum.122), channel_id=1, replica_groups=mesh['wide_0'=4,'wide_1'=4,'wide_2'=2,'narrow'=8] {'narrow'}, use_global_device_ids=true, to_apply=%region_19.20 | all-reduce | flops 1 | bytes 8 | tf_op jit(solution)/shard_map/psum | solution.py:34
  217.4 5.6 %collective-permute-start.8 = (f32[2,64,256]{2,1,0:T(8,128)S(1)}, f32[2,64,256]{2,1,0:T(8,128)S(1)}, u32[]{:S(2)}, u32[]{:S(2)}) collective-permute-start(f32[2,64,256]{2,1,0:T(8,128)S(1)} %get-tuple-element.600), channel_id=1, source_target_pairs={{0,8},{8,16},{16,24},{24,32},{32,40},{40,48},{48,56},{56,64},{64,7... | collective-permute-start | bytes 393224 | tf_op jit(solution)/shard_map/ppermute | solution.py:27
  234.4 5.0 %collective-permute-done.10 = f32[2,384,64]{2,1,0:T(8,128)S(1)} collective-permute-done((f32[2,384,64]{2,1,0:T(8,128)S(1)}, f32[2,384,64]{2,1,0:T(8,128)S(1)}, u32[]{:S(2)}, u32[]{:S(2)}) %collective-permute-start.10) | collective-permute-done | bytes 196640 | tf_op jit(solution)/shard_map/ppermute | solution.py:27
  246.2 48.1 %while.39 = (s32[]{:T(128)}, f32[2,384,384]{2,1,0:T(8,128)}, s32[]{:T(128)}, s32[1,1,3,2]{2,3,1,0:T(2,128)S(1)}, bf16[4,2,256,256]{3,2,0,1:T(8,128)(2,1)S(1)}, /...) while((s32[]{:T(128)}, f32[2,384,384]{2,1,0:T(8,128)}, ...), condition=%wide.region_24.25_spmd, body=%wide.region_20.0_spmd.sunk | while | flops 2158034944 | bytes 27525440 | solution.py:162
  263.6 6.3 %dynamic_update_slice.19 = f32[2,384,384]{2,1,0:T(8,128)} dynamic-update-slice(f32[2,384,384]{2,1,0:T(8,128)} %get-tuple-element.853, f32[2,256,256]{2,1,0:T(8,128)S(1)} %fusion.136, s32[]{:T(128)} %constant.314.clone.1..sunk.1, s32[]{:T(128)S(6)} %select_n.151, s32[]{:T(128)S(6)} %select_n.152) | dynamic-update-slice | bytes 1048580 | tf_op jit(solution)/shard_map/while/body/dynamic_update_slice | solution.py:157
  287.4 6.2 %dynamic_update_slice.19 = f32[2,384,384]{2,1,0:T(8,128)} dynamic-update-slice(f32[2,384,384]{2,1,0:T(8,128)} %get-tuple-element.853, f32[2,256,256]{2,1,0:T(8,128)S(1)} %fusion.136, s32[]{:T(128)} %constant.314.clone.1..sunk.1, s32[]{:T(128)S(6)} %select_n.151, s32[]{:T(128)S(6)} %select_n.152) | dynamic-update-slice | bytes 1048580 | tf_op jit(solution)/shard_map/while/body/dynamic_update_slice | solution.py:157
  305.6 26.0 %collective-permute-start.14 = (f32[2,256,64]{2,1,0:T(8,128)S(1)}, f32[2,256,64]{2,1,0:T(8,128)S(1)}, u32[]{:S(2)}, u32[]{:S(2)}) collective-permute-start(f32[2,256,64]{2,1,0:T(8,128)S(1)} %get-tuple-element.593), channel_id=1, source_target_pairs={{0,1},{1,2},{2,3},{3,4},{4,5},{5,6},{6,7},{8,9},{9,10},{10,11},{11... | collective-permute-start | bytes 393224 | tf_op jit(solution)/shard_map/ppermute | solution.py:27
  341.6 11.1 %psum.124 = f32[]{:T(128)} all-reduce(f32[]{:T(128)} %multiply_reduce_fusion), channel_id=1, replica_groups=mesh['wide_0'=4,'wide_1'=4,'wide_2'=2,'narrow'=8] {'wide_0'}, use_global_device_ids=true, to_apply=%region_26.27 | all-reduce | flops 1 | bytes 8 | tf_op jit(solution)/shard_map/psum | solution.py:34
  352.7 10.5 %psum.125 = f32[]{:T(128)} all-reduce(f32[]{:T(128)} %psum.124), channel_id=1, replica_groups=mesh['wide_0'=4,'wide_1'=4,'wide_2'=2,'narrow'=8] {'wide_1'}, use_global_device_ids=true, to_apply=%region_27.28 | all-reduce | flops 1 | bytes 8 | tf_op jit(solution)/shard_map/psum | solution.py:34
  363.2 5.0 %psum.126 = f32[]{:T(128)} all-reduce(f32[]{:T(128)} %psum.125), channel_id=1, replica_groups=mesh['wide_0'=4,'wide_1'=4,'wide_2'=2,'narrow'=8] {'wide_2'}, use_global_device_ids=true, to_apply=%region_28.29 | all-reduce | flops 1 | bytes 8 | tf_op jit(solution)/shard_map/psum | solution.py:34
  368.1 13.6 %psum.127 = f32[]{:T(128)} all-reduce(f32[]{:T(128)} %psum.126), channel_id=1, replica_groups=mesh['wide_0'=4,'wide_1'=4,'wide_2'=2,'narrow'=8] {'narrow'}, use_global_device_ids=true, to_apply=%region_29.30 | all-reduce | flops 1 | bytes 8 | tf_op jit(solution)/shard_map/psum | solution.py:34
  (143 shorter events, 145.9 us)
Async XLA Ops:
  1.6 16.0 %collective-permute-start = (f32[2,64,256]{2,1,0:T(8,128)S(1)}, f32[2,64,256]{2,1,0:T(8,128)S(1)}, u32[]{:S(2)}, u32[]{:S(2)}) collective-permute-start(f32[2,64,256]{2,1,0:T(8,128)S(1)} %get-tuple-element.603), channel_id=1, source_target_pairs={{0,8},{8,16},{16,24},{24,32},{32,40},{40,48},{48,56},{56,64},{64,7... | collective-permute-start | bytes 393224 | tf_op jit(solution)/shard_map/ppermute | solution.py:27
  6.2 12.4 %collective-permute-start.1 = (f32[2,64,256]{2,1,0:T(8,128)S(1)}, f32[2,64,256]{2,1,0:T(8,128)S(1)}, u32[]{:S(2)}, u32[]{:S(2)}) collective-permute-start(f32[2,64,256]{2,1,0:T(8,128)S(1)} %get-tuple-element.602), channel_id=1, source_target_pairs={{8,0},{16,8},{24,16},{32,24},{40,32},{48,40},{56,48},{64,56},{72,6... | collective-permute-start | bytes 393224 | tf_op jit(solution)/shard_map/ppermute | solution.py:28
  13.3 2.3 copy-start.7
  15.5 2.0 copy-start.8
  18.8 11.0 %collective-permute-start.2 = (f32[2,384,64]{2,1,0:T(8,128)S(1)}, f32[2,384,64]{2,1,0:T(8,128)S(1)}, u32[]{:S(2)}, u32[]{:S(2)}) collective-permute-start(f32[2,384,64]{2,1,0:T(8,128)S(1)} %get-tuple-element.598), channel_id=1, source_target_pairs={{0,1},{1,2},{2,3},{3,4},{4,5},{5,6},{6,7},{8,9},{9,10},{10,11},{11... | collective-permute-start | bytes 589832 | tf_op jit(solution)/shard_map/ppermute | solution.py:27
  22.4 11.5 %collective-permute-start.3 = (f32[2,384,64]{2,1,0:T(8,128)S(1)}, f32[2,384,64]{2,1,0:T(8,128)S(1)}, u32[]{:S(2)}, u32[]{:S(2)}) collective-permute-start(f32[2,384,64]{2,1,0:T(8,128)S(1)} %get-tuple-element.599), channel_id=1, source_target_pairs={{1,0},{2,1},{3,2},{4,3},{5,4},{6,5},{7,6},{9,8},{10,9},{11,10},{12... | collective-permute-start | bytes 589832 | tf_op jit(solution)/shard_map/ppermute | solution.py:28
  85.3 5.5 %collective-permute-start.4 = (f32[2,64,384]{2,1,0:T(8,128)S(1)}, f32[2,64,384]{2,1,0:T(8,128)S(1)}, u32[]{:S(2)}, u32[]{:S(2)}) collective-permute-start(f32[2,64,384]{2,1,0:T(8,128)S(1)} %get-tuple-element.589), channel_id=1, source_target_pairs={{0,8},{8,16},{16,24},{24,32},{32,40},{40,48},{48,56},{56,64},{64,7... | collective-permute-start | bytes 589832 | tf_op jit(solution)/shard_map/ppermute | solution.py:27
  88.5 7.0 %collective-permute-start.5 = (f32[2,64,384]{2,1,0:T(8,128)S(1)}, f32[2,64,384]{2,1,0:T(8,128)S(1)}, u32[]{:S(2)}, u32[]{:S(2)}) collective-permute-start(f32[2,64,384]{2,1,0:T(8,128)S(1)} %get-tuple-element.588), channel_id=1, source_target_pairs={{8,0},{16,8},{24,16},{32,24},{40,32},{48,40},{56,48},{64,56},{72,6... | collective-permute-start | bytes 589832 | tf_op jit(solution)/shard_map/ppermute | solution.py:28
  95.6 30.0 %collective-permute-start.6 = (f32[2,256,64]{2,1,0:T(8,128)S(1)}, f32[2,256,64]{2,1,0:T(8,128)S(1)}, u32[]{:S(2)}, u32[]{:S(2)}) collective-permute-start(f32[2,256,64]{2,1,0:T(8,128)S(1)} %get-tuple-element.597), channel_id=1, source_target_pairs={{0,1},{1,2},{2,3},{3,4},{4,5},{5,6},{6,7},{8,9},{9,10},{10,11},{11... | collective-permute-start | bytes 393224 | tf_op jit(solution)/shard_map/ppermute | solution.py:27
  122.6 9.0 %copy-start.1 = (f32[2,256,256]{2,1,0:T(8,128)S(1)}, f32[2,256,256]{2,1,0:T(8,128)}, u32[]{:S(2)}) copy-start(f32[2,256,256]{2,1,0:T(8,128)} %param.25) | copy-start | bytes 1572868
  122.6 7.6 %collective-permute-start.7 = (f32[2,256,64]{2,1,0:T(8,128)S(1)}, f32[2,256,64]{2,1,0:T(8,128)S(1)}, u32[]{:S(2)}, u32[]{:S(2)}) collective-permute-start(f32[2,256,64]{2,1,0:T(8,128)S(1)} %get-tuple-element.596), channel_id=1, source_target_pairs={{1,0},{2,1},{3,2},{4,3},{5,4},{6,5},{7,6},{9,8},{10,9},{11,10},{12... | collective-permute-start | bytes 393224 | tf_op jit(solution)/shard_map/ppermute | solution.py:28
  131.6 85.7 %copy-start.3 = (f32[2,256,256]{2,1,0:T(8,128)}, f32[2,256,256]{2,1,0:T(8,128)S(1)}, u32[]{:S(2)}) copy-start(f32[2,256,256]{2,1,0:T(8,128)S(1)} %scatter-add.31) | copy-start | bytes 1572868
  217.3 26.3 %copy-start.5 = (f32[2,256,256]{2,1,0:T(8,128)}, f32[2,256,256]{2,1,0:T(8,128)S(1)}, u32[]{:S(2)}) copy-start(f32[2,256,256]{2,1,0:T(8,128)S(1)} %multiply_add_fusion.2) | copy-start | bytes 1572868
  217.4 7.5 %collective-permute-start.8 = (f32[2,64,256]{2,1,0:T(8,128)S(1)}, f32[2,64,256]{2,1,0:T(8,128)S(1)}, u32[]{:S(2)}, u32[]{:S(2)}) collective-permute-start(f32[2,64,256]{2,1,0:T(8,128)S(1)} %get-tuple-element.600), channel_id=1, source_target_pairs={{0,8},{8,16},{16,24},{24,32},{32,40},{40,48},{48,56},{56,64},{64,7... | collective-permute-start | bytes 393224 | tf_op jit(solution)/shard_map/ppermute | solution.py:27
  223.0 6.3 %collective-permute-start.9 = (f32[2,64,256]{2,1,0:T(8,128)S(1)}, f32[2,64,256]{2,1,0:T(8,128)S(1)}, u32[]{:S(2)}, u32[]{:S(2)}) collective-permute-start(f32[2,64,256]{2,1,0:T(8,128)S(1)} %get-tuple-element.601), channel_id=1, source_target_pairs={{8,0},{16,8},{24,16},{32,24},{40,32},{48,40},{56,48},{64,56},{72,6... | collective-permute-start | bytes 393224 | tf_op jit(solution)/shard_map/ppermute | solution.py:28
  229.5 10.0 %collective-permute-start.10 = (f32[2,384,64]{2,1,0:T(8,128)S(1)}, f32[2,384,64]{2,1,0:T(8,128)S(1)}, u32[]{:S(2)}, u32[]{:S(2)}) collective-permute-start(f32[2,384,64]{2,1,0:T(8,128)S(1)} %get-tuple-element.594), channel_id=1, source_target_pairs={{0,1},{1,2},{2,3},{3,4},{4,5},{5,6},{6,7},{8,9},{9,10},{10,11},{11... | collective-permute-start | bytes 589832 | tf_op jit(solution)/shard_map/ppermute | solution.py:27
  233.1 10.4 %collective-permute-start.11 = (f32[2,384,64]{2,1,0:T(8,128)S(1)}, f32[2,384,64]{2,1,0:T(8,128)S(1)}, u32[]{:S(2)}, u32[]{:S(2)}) collective-permute-start(f32[2,384,64]{2,1,0:T(8,128)S(1)} %get-tuple-element.595), channel_id=1, source_target_pairs={{1,0},{2,1},{3,2},{4,3},{5,4},{6,5},{7,6},{9,8},{10,9},{11,10},{12... | collective-permute-start | bytes 589832 | tf_op jit(solution)/shard_map/ppermute | solution.py:28
  295.3 5.5 %collective-permute-start.12 = (f32[2,64,384]{2,1,0:T(8,128)S(1)}, f32[2,64,384]{2,1,0:T(8,128)S(1)}, u32[]{:S(2)}, u32[]{:S(2)}) collective-permute-start(f32[2,64,384]{2,1,0:T(8,128)S(1)} %get-tuple-element.587), channel_id=1, source_target_pairs={{0,8},{8,16},{16,24},{24,32},{32,40},{40,48},{48,56},{56,64},{64,7... | collective-permute-start | bytes 589832 | tf_op jit(solution)/shard_map/ppermute | solution.py:27
  298.5 7.0 %collective-permute-start.13 = (f32[2,64,384]{2,1,0:T(8,128)S(1)}, f32[2,64,384]{2,1,0:T(8,128)S(1)}, u32[]{:S(2)}, u32[]{:S(2)}) collective-permute-start(f32[2,64,384]{2,1,0:T(8,128)S(1)} %get-tuple-element.586), channel_id=1, source_target_pairs={{8,0},{16,8},{24,16},{32,24},{40,32},{48,40},{56,48},{64,56},{72,6... | collective-permute-start | bytes 589832 | tf_op jit(solution)/shard_map/ppermute | solution.py:28
  305.6 29.4 %collective-permute-start.14 = (f32[2,256,64]{2,1,0:T(8,128)S(1)}, f32[2,256,64]{2,1,0:T(8,128)S(1)}, u32[]{:S(2)}, u32[]{:S(2)}) collective-permute-start(f32[2,256,64]{2,1,0:T(8,128)S(1)} %get-tuple-element.593), channel_id=1, source_target_pairs={{0,1},{1,2},{2,3},{3,4},{4,5},{5,6},{6,7},{8,9},{9,10},{10,11},{11... | collective-permute-start | bytes 393224 | tf_op jit(solution)/shard_map/ppermute | solution.py:27
  331.8 9.0 %copy-start.6 = (f32[2,256,256]{2,1,0:T(8,128)S(1)}, f32[2,256,256]{2,1,0:T(8,128)}, u32[]{:S(2)}) copy-start(f32[2,256,256]{2,1,0:T(8,128)} %copy-done.5) | copy-start | bytes 1572868
  331.8 7.6 %collective-permute-start.15 = (f32[2,256,64]{2,1,0:T(8,128)S(1)}, f32[2,256,64]{2,1,0:T(8,128)S(1)}, u32[]{:S(2)}, u32[]{:S(2)}) collective-permute-start(f32[2,256,64]{2,1,0:T(8,128)S(1)} %get-tuple-element.592), channel_id=1, source_target_pairs={{1,0},{2,1},{3,2},{4,3},{5,4},{6,5},{7,6},{9,8},{10,9},{11,10},{12... | collective-permute-start | bytes 393224 | tf_op jit(solution)/shard_map/ppermute | solution.py:28
  336.3 46.7 %copy-start.2 = (f32[2,256,256]{2,1,0:T(8,128)S(1)}, f32[2,256,256]{2,1,0:T(8,128)}, u32[]{:S(2)}) copy-start(f32[2,256,256]{2,1,0:T(8,128)} %param.25) | copy-start | bytes 1572868
  336.3 46.7 %copy-start.4 = (f32[2,256,256]{2,1,0:T(8,128)S(1)}, f32[2,256,256]{2,1,0:T(8,128)}, u32[]{:S(2)}) copy-start(f32[2,256,256]{2,1,0:T(8,128)} %copy-done.3) | copy-start | bytes 1572868
  (2 other events, 2.1 us)
where the time goes:
time: 391 us; the launch traced here: 384 us
  blocking collectives  122 us (31%)
  starting transfers between devices  88.1 us (23%)
  local copies, waits for them, and re-layouts  56.1 us (14%)
  waiting for transfers between devices  39.1 us (10%)
  other arithmetic  37.6 us (10%)
  matrix products  22.4 us (6%)
  loops' own time  14.3 us (4%)
  between operations  4.77 us (1%)
    psum x12, blocking collectives, one_axis_at_a_time(): return functools.reduce(lax.psum, axes, x)  122 us
    ppermute x8, starting transfers between devices, padded(): before = lax.ppermute(last, axis, up)  74 us
    ppermute x8, waiting for transfers between devices, padded(): after = lax.ppermute(initial, axis, down)  26.3 us
    dynamic_update_slice x4, local copies, waits for them, and re-layouts, visit(): lax.dynamic_update_slice(running, region + contribution[0], (0, row_start...  25.1 us
    dot_general x8, matrix products, right_apply(): jnp.einsum('nqac,qpcd->npad', values, table, preferred_element_type=jnp.f...  22.4 us
    another operation x2, loops' own time, apply_operator(): lax.fori_loop(0, counts[0, 0], visit, (total, jnp.float32(0.0)))  14.3 us
    ppermute x8, starting transfers between devices, padded(): after = lax.ppermute(initial, axis, down)  14.1 us
    ppermute x8, waiting for transfers between devices, padded(): before = lax.ppermute(last, axis, up)  12.7 us
  transfers between devices with their start and end apart: 16, of which 11 were waited for; matrix products, arithmetic and copies ran while one was open for 5% of the time, Pallas kernels for 0%

commit v1 on v0

v1 whole, which is shorter than its diff:
```python
import functools
import math

import jax
import jax.numpy as jnp
import numpy as np
from jax import lax
from jax.experimental import pallas as pl
from jax.experimental.pallas import tpu as pltpu
from jax.sharding import PartitionSpec as P

W = 256
MODES = 4
FCAP = 3
HALO = 64
EXT = W + 2 * HALO
LANES = 128
DAMPING = 0.5
MESH = pl.DeviceIdType.MESH
F32 = jnp.float32
BF16 = jnp.bfloat16


def tables():
    counter = np.arange(W)
    angles = (counter[:, None] * counter[None, :] % W) * (2.0 * math.pi / W)
    re = np.cos(angles) / math.sqrt(W)
    s = np.sin(angles) / math.sqrt(W)
    ahead = np.block([[re, s], [-s, re]])
    back = np.block([[re, -s], [s, re]])
    return np.stack([ahead, back]).astype(jnp.bfloat16)


def kernel(
    wide,
    narrow,
    offs,
    counts,
    tab_hbm,
    grad_hbm,
    probe_hbm,
    weight_hbm,
    sol_ref,
    res_ref,
    grad,
    tab,
    probe,
    weight,
    ext,
    side,
    acc,
    acc_side,
    image,
    packs,
    rows_in,
    sides_in,
    patch,
    waves,
    parts,
    proj,
    pad,
    ar_src,
    ar_z,
    ar_w,
    load_sems,
    x_send,
    x_recv,
    ar_send,
    ar_recv,
):
    me_w, me_n = lax.axis_index("wide"), lax.axis_index("narrow")

    def dev(w, n):
        return (lax.rem(w, wide), lax.rem(n, narrow))

    up, down = me_w + wide - 1, me_w + 1
    left, right = me_n + narrow - 1, me_n + 1

    loads = [
        pltpu.make_async_copy(grad_hbm, grad, load_sems.at[0]),
        pltpu.make_async_copy(tab_hbm, tab, load_sems.at[1]),
        pltpu.make_async_copy(probe_hbm, probe, load_sems.at[2]),
        pltpu.make_async_copy(weight_hbm.at[0, 0], weight, load_sems.at[3]),
    ]
    for load in loads:
        load.start()

    barrier = pltpu.get_barrier_semaphore()

    def greet_w(i, c):
        pl.semaphore_signal(barrier, inc=1, device_id=dev(me_w + i, me_n), device_id_type=MESH)
        return c

    def greet_n(i, c):
        pl.semaphore_signal(barrier, inc=1, device_id=dev(me_w, me_n + i), device_id_type=MESH)
        return c

    for w in (up, down):
        for n in (left, right):
            pl.semaphore_signal(barrier, inc=1, device_id=dev(w, n), device_id_type=MESH)
    lax.fori_loop(1, narrow, greet_n, 0)
    lax.fori_loop(1, wide, greet_w, 0)

    lane = lax.broadcasted_iota(jnp.int32, (1, LANES), 1)
    low = lane < HALO

    def pack_halo(src, k):
        re0, im0 = src[0, :, :LANES], src[1, :, :LANES]
        re1, im1 = src[0, :, LANES:], src[1, :, LANES:]
        packs[k, 0, HALO : HALO + W, :] = jnp.where(low, re0, pltpu.roll(im0, HALO, 1))
        packs[k, 1, HALO : HALO + W, :] = jnp.where(low, pltpu.roll(im1, HALO, 1), re1)

    def exchange(k, row_up, row_down, corner_up, corner_down):
        mid = pl.ds(HALO, W)
        first, last = pl.ds(0, HALO), pl.ds(HALO + W, HALO)
        plan = [
            (packs.at[k, 0, mid], sides_in.at[k, 1, mid], (me_w, left)),
            (packs.at[k, 1, mid], sides_in.at[k, 0, mid], (me_w, right)),
            (row_up, rows_in.at[k, 1], (up, me_n)),
            (row_down, rows_in.at[k, 0], (down, me_n)),
            (packs.at[k, 0, corner_up], sides_in.at[k, 1, last], (up, left)),
            (packs.at[k, 1, corner_up], sides_in.at[k, 0, last], (up, right)),
            (packs.at[k, 0, corner_down], sides_in.at[k, 1, first], (down, left)),
            (packs.at[k, 1, corner_down], sides_in.at[k, 0, first], (down, right)),
        ]
        copies = [
            pltpu.make_async_remote_copy(
                src_ref=src,
                dst_ref=dst,
                send_sem=x_send.at[k, j],
                recv_sem=x_recv.at[k, j],
                device_id=dev(*where),
                device_id_type=MESH,
            )
            for j, (src, dst, where) in enumerate(plan)
        ]
        for copy in copies:
            copy.start()
        return copies

    def halo_exchange(k, src):
        return exchange(
            k,
            src.at[:, pl.ds(0, HALO)],
            src.at[:, pl.ds(W - HALO, HALO)],
            pl.ds(HALO, HALO),
            pl.ds(W, HALO),
        )

    def fold_exchange(k, step):
        return exchange(
            k,
            acc.at[step, :, pl.ds(0, HALO)],
            acc.at[step, :, pl.ds(HALO + W, HALO)],
            pl.ds(0, HALO),
            pl.ds(HALO + W, HALO),
        )

    has_up = (me_w > 0).astype(F32)
    has_down = (me_w < wide - 1).astype(F32)
    has_left = (me_n > 0).astype(F32)
    has_right = (me_n < narrow - 1).astype(F32)

    def unpacked_halo(k):
        scale = jnp.where(low, has_right, has_left)
        lf, rt = sides_in[k, 0], sides_in[k, 1]
        re = jnp.where(low, rt, lf) * scale
        im = pltpu.roll(jnp.where(low, lf, rt), HALO, 1) * scale
        return re, im

    def ar_start(a, value):
        ar_src[a, 0] = value
        ar_z[a, me_n] = value

        def send(i, c):
            pltpu.make_async_remote_copy(
                src_ref=ar_src.at[a, 0],
                dst_ref=ar_z.at[a, me_n],
                send_sem=ar_send.at[a, 0],
                recv_sem=ar_recv.at[a, 0],
                device_id=dev(me_w, me_n + i),
                device_id_type=MESH,
            ).start()
            return c

        lax.fori_loop(1, narrow, send, 0)

    def ar_middle(a):
        some = ar_z.at[a, pl.ds(0, narrow - 1)]
        pltpu.make_async_copy(some, some, ar_recv.at[a, 0]).wait()
        value = jnp.sum(ar_z[a], axis=0)
        ar_src[a, 1] = value
        ar_w[a, me_w] = value

        def send(i, c):
            pltpu.make_async_remote_copy(
                src_ref=ar_src.at[a, 1],
                dst_ref=ar_w.at[a, me_w],
                send_sem=ar_send.at[a, 1],
                recv_sem=ar_recv.at[a, 1],
                device_id=dev(me_w + i, me_n),
                device_id_type=MESH,
            ).start()
            return c

        lax.fori_loop(1, wide, send, 0)

    def ar_finish(a):
        some = ar_w.at[a, pl.ds(0, wide - 1)]
        pltpu.make_async_copy(some, some, ar_recv.at[a, 1]).wait()
        total = jnp.sum(ar_w[a], axis=0)
        total = jnp.sum(total, axis=1, keepdims=True)
        return total[0:1], total[1:2]

    def ar_drain(a):
        some = ar_z.at[a, pl.ds(0, narrow - 1)]
        pltpu.make_async_copy(some, some, ar_send.at[a, 0]).wait()
        some = ar_w.at[a, pl.ds(0, wide - 1)]
        pltpu.make_async_copy(some, some, ar_send.at[a, 1]).wait()

    def squares(x):
        s = jnp.sum(x * x, axis=0, keepdims=True)
        return s[:, :LANES] + s[:, LANES:]

    count = counts[0, 0]
    halves = (slice(0, LANES), slice(LANES, W))

    def forward(step):
        def frame(f, total):
            o0, o1 = offs[0, 0, f, 0], offs[0, 0, f, 1]
            own = (lane + o1 >= 0) & (lane + o1 < LANES)
            shift = lax.rem(LANES - o1, LANES)
            window = pl.ds(HALO + o0, W)
            for q in range(2):
                strip = side[step, q, window, :]
                a = jnp.where(lane < o1, strip, ext[step, q, 0, window, :])
                b = jnp.where(lane >= LANES + o1, strip, ext[step, q, 1, window, :])
                a, b = pltpu.roll(a, shift, 1), pltpu.roll(b, shift, 1)
                patch[q, :, :LANES] = jnp.where(own, a, b)
                patch[q, :, LANES:] = jnp.where(own, b, a)
            for m in range(MODES):
                pr, pi = probe[m, 0].astype(F32), probe[m, 1].astype(F32)
                xr, xi = patch[0], patch[1]
                waves[m, :W] = (pr * xr - pi * xi).astype(BF16)
                waves[m, W:] = (pr * xi + pi * xr).astype(BF16)
                part = jnp.dot(tab[0], waves[m], preferred_element_type=F32).astype(BF16)
                parts[m, :, :W] = part[:W]
                parts[m, :, W:] = part[W:]
                far = jnp.dot(parts[m], tab[1], preferred_element_type=F32)
                term = weight[f, m, 0].astype(F32) * far[:, :W] + weight[f, m, 1].astype(F32) * far[:, W:]
                if m == 0:
                    proj[f] = term
                else:
                    proj[f] += term
            live = (f < count).astype(F32)
            p = proj[f] * live
            proj[f] = p
            return total + squares(p)

        return lax.fori_loop(0, FCAP, frame, jnp.zeros((1, LANES), F32))

    def backward_frame(step, f):
        o0, o1 = offs[0, 0, f, 0], offs[0, 0, f, 1]
        p = proj[f]
        for m in range(MODES):
            waves[m, :W] = (weight[f, m, 0].astype(F32) * p).astype(BF16)
            waves[m, W:] = (weight[f, m, 1].astype(F32) * p).astype(BF16)
            part = jnp.dot(tab[1], waves[m], preferred_element_type=F32).astype(BF16)
            parts[m, :, :W] = part[:W]
            parts[m, :, W:] = part[W:]
            near = jnp.dot(parts[m], tab[0], preferred_element_type=F32)
            pr, pi = probe[m, 0].astype(F32), probe[m, 1].astype(F32)
            nr, ni = near[:, :W], near[:, W:]
            if m == 0:
                patch[0] = pr * nr + pi * ni
                patch[1] = pr * ni - pi * nr
            else:
                patch[0] += pr * nr + pi * ni
                patch[1] += pr * ni - pi * nr
        own = (lane - o1 >= 0) & (lane - o1 < LANES)
        shift = lax.rem(LANES + o1, LANES)
        window = pl.ds(HALO - o0, EXT)
        to_right, to_left = lane < o1, lane >= LANES + o1
        for q in range(2):
            a = pltpu.roll(patch[q, :, :LANES], shift, 1)
            b = pltpu.roll(patch[q, :, LANES:], shift, 1)
            pad[q, 0, 2 * HALO : 2 * HALO + W, :] = jnp.where(own, a, b)
            pad[q, 1, 2 * HALO : 2 * HALO + W, :] = jnp.where(own, b, a)
            a, b = pad[q, 0, window, :], pad[q, 1, window, :]
            acc[step, q, :, :LANES] += jnp.where(to_right, 0.0, a)
            acc[step, q, :, LANES:] += jnp.where(to_left, 0.0, b)
            acc_side[q] += jnp.where(to_right, a, jnp.where(to_left, b, 0.0))

    def backward(step):
        def frame(f, c):
            backward_frame(step, f)
            return c

        lax.fori_loop(1, FCAP, frame, 0)

    def pack_fold(k):
        re, im = acc_side[0], pltpu.roll(acc_side[1], HALO, 1)
        packs[k, 1] = jnp.where(low, re, im)
        packs[k, 0] = jnp.where(low, im, re)

    def fold_in(k, step):
        for q in range(2):
            for h in range(2):
                own = acc[step, q, HALO : HALO + W, halves[h]]
                image[q, :, halves[h]] = own + DAMPING * ext[step, q, h, HALO : HALO + W, :]
            image[q, :HALO, :] += rows_in[k, 0, q] * has_up
            image[q, W - HALO :, :] += rows_in[k, 1, q] * has_down
        lf, rt = sides_in[k, 0], sides_in[k, 1]
        for rows, piece, scale in (
            (slice(0, W), slice(HALO, HALO + W), 1.0),
            (slice(0, HALO), slice(0, HALO), has_up),
            (slice(W - HALO, W), slice(HALO + W, EXT), has_down),
        ):
            l, r = lf[piece] * (has_left * scale), rt[piece] * (has_right * scale)
            image[0, rows, :LANES] += jnp.where(low, l, 0.0)
            image[0, rows, LANES:] += jnp.where(low, 0.0, r)
            image[1, rows, :LANES] += jnp.where(low, pltpu.roll(l, HALO, 1), 0.0)
            image[1, rows, LANES:] += jnp.where(low, 0.0, pltpu.roll(r, HALO, 1))

    loads[0].wait()
    pack_halo(grad, 0)
    pl.semaphore_wait(barrier, wide + narrow + 2)
    x0 = halo_exchange(0, grad)

    pad[...] = jnp.zeros_like(pad)
    acc[...] = jnp.zeros_like(acc)
    acc_side[...] = jnp.zeros_like(acc_side)
    norm = jnp.zeros((1, LANES), F32)
    for q in range(2):
        for h in range(2):
            ext[0, q, h, HALO : HALO + W, :] = grad[q, :, halves[h]]
        norm += squares(grad[q])
    for load in loads[1:]:
        load.wait()

    for copy in x0:
        copy.wait_recv()
    ends = ((slice(0, HALO), 0, has_up), (slice(HALO + W, EXT), 1, has_down))
    for rows, e, scale in ends:
        for q in range(2):
            for h in range(2):
                ext[0, q, h, rows, :] = rows_in[0, e, q, :, halves[h]] * scale
    halo = unpacked_halo(0)
    for q in range(2):
        side[0, q] = halo[q]
        for rows, e, scale in ends:
            side[0, q, rows, :] = side[0, q, rows, :] * scale

    total = forward(0) + DAMPING * norm
    ar_start(0, jnp.concatenate([norm, total], axis=0))
    backward_frame(0, 0)
    ar_middle(0)
    backward(0)
    pack_fold(1)
    x1 = fold_exchange(1, 0)
    for copy in x1:
        copy.wait_recv()
    fold_in(1, 0)
    pack_halo(image, 2)
    x2 = halo_exchange(2, image)
    acc_side[...] = jnp.zeros_like(acc_side)

    norm0, curvature = ar_finish(0)
    alpha0 = norm0 / curvature
    norm = jnp.zeros((1, LANES), F32)
    for q in range(2):
        r = grad[q] - alpha0 * image[q]
        res_ref[q] = r
        norm += squares(r)
    ar_start(1, jnp.concatenate([norm, norm], axis=0))
    for copy in x2:
        copy.wait_recv()
    ar_middle(1)
    halo = unpacked_halo(2)
    for q in range(2):
        side[1, q] = side[0, q] - alpha0 * halo[q]
        for rows, e, scale in ends:
            for h in range(2):
                ext[1, q, h, rows, :] = ext[0, q, h, rows, :] - alpha0 * rows_in[2, e, q, :, halves[h]]
    norm1, _ = ar_finish(1)
    beta = norm1 / norm0
    norm = jnp.zeros((1, LANES), F32)
    for q in range(2):
        for h in range(2):
            d = res_ref[q, :, halves[h]] + beta * grad[q, :, halves[h]]
            ext[1, q, h, HALO : HALO + W, :] = d
            norm += jnp.sum(d * d, axis=0, keepdims=True)
        side[1, q] = side[1, q] + beta * side[0, q]
        for rows, e, scale in ends:
            for h in range(2):
                ext[1, q, h, rows, :] = (ext[1, q, h, rows, :] + beta * ext[0, q, h, rows, :]) * scale
            side[1, q, rows, :] = side[1, q, rows, :] * scale

    total = forward(1) + DAMPING * norm
    ar_start(2, jnp.concatenate([total, total], axis=0))
    backward_frame(1, 0)
    ar_middle(2)
    backward(1)
    pack_fold(3)
    x3 = fold_exchange(3, 1)
    for copy in x2:
        copy.wait_send()
    for copy in x3:
        copy.wait_recv()
    fold_in(3, 1)
    curvature, _ = ar_finish(2)
    alpha1 = norm1 / curvature
    for q in range(2):
        for h in range(2):
            sol_ref[q, :, halves[h]] = alpha0 * grad[q, :, halves[h]] + alpha1 * ext[1, q, h, HALO : HALO + W, :]
        res_ref[q] = res_ref[q] - alpha1 * image[q]

    for copy in x0 + x1 + x3:
        copy.wait_send()
    for a in range(3):
        ar_drain(a)


def solution(mesh):
    wide, narrow = mesh.shape["wide"], mesh.shape["narrow"]
    tab = tables()
    tile = jax.ShapeDtypeStruct((2, W, W), F32)
    hbm = pl.BlockSpec(memory_space=pl.ANY)
    smem = pl.BlockSpec(memory_space=pltpu.SMEM)
    vmem = pl.BlockSpec(memory_space=pltpu.VMEM)

    def local(gradient, probe_modes, mode_weights, offsets, counts):
        return pl.pallas_call(
            functools.partial(kernel, wide, narrow),
            out_shape=(tile, tile),
            in_specs=[smem, smem, hbm, hbm, hbm, hbm],
            out_specs=(vmem, vmem),
            scratch_shapes=[
                pltpu.VMEM((2, W, W), F32),
                pltpu.VMEM((2, 2 * W, 2 * W), BF16),
                pltpu.VMEM((MODES, 2, W, W), BF16),
                pltpu.VMEM((FCAP, MODES, 2, W, W), BF16),
                pltpu.VMEM((2, 2, 2, EXT, LANES), F32),
                pltpu.VMEM((2, 2, EXT, LANES), F32),
                pltpu.VMEM((2, 2, EXT, W), F32),
                pltpu.VMEM((2, EXT, LANES), F32),
                pltpu.VMEM((2, W, W), F32),
                pltpu.VMEM((4, 2, EXT, LANES), F32),
                pltpu.VMEM((4, 2, 2, HALO, W), F32),
                pltpu.VMEM((4, 2, EXT, LANES), F32),
                pltpu.VMEM((2, W, W), F32),
                pltpu.VMEM((MODES, 2 * W, W), BF16),
                pltpu.VMEM((MODES, W, 2 * W), BF16),
                pltpu.VMEM((FCAP, W, W), F32),
                pltpu.VMEM((2, 2, EXT + 2 * HALO, LANES), F32),
                pltpu.VMEM((3, 2, 2, LANES), F32),
                pltpu.VMEM((3, narrow, 2, LANES), F32),
                pltpu.VMEM((3, wide, 2, LANES), F32),
                pltpu.SemaphoreType.DMA((4,)),
                pltpu.SemaphoreType.DMA((4, 8)),
                pltpu.SemaphoreType.DMA((4, 8)),
                pltpu.SemaphoreType.DMA((3, 2)),
                pltpu.SemaphoreType.DMA((3, 2)),
            ],
            compiler_params=pltpu.CompilerParams(
                collective_id=0, has_side_effects=True, vmem_limit_bytes=60 * 1024 * 1024
            ),
        )(offsets, counts, jnp.asarray(tab), gradient, probe_modes, mode_weights)

    spec = P(None, "wide", "narrow")
    return jax.shard_map(
        local,
        mesh=mesh,
        in_specs=(
            spec,
            P(),
            P("wide", "narrow", None, None, None, None, None),
            P("wide", "narrow", None, None),
            P("wide", "narrow"),
        ),
        out_specs=(spec, spec),
        check_vma=False,
    )
```

time: 391 us -> 82 us (0.21); the launches traced: 384 us -> 81.8 us
  blocking collectives: 122 us -> 0 us
  starting transfers between devices: 88.1 us -> 0 us
  Pallas kernels: 0 us -> 75.4 us
  local copies, waits for them, and re-layouts: 56.1 us -> 5.07 us
  waiting for transfers between devices: 39.1 us -> 0 us
  other arithmetic: 37.6 us -> 0 us
  matrix products: 22.4 us -> 0 us
  loops' own time: 14.3 us -> 0 us
    psum x12 -> x0, blocking collectives: 122 us -> none  [one_axis_at_a_time(): return functools.reduce(lax.psum, axes, x)]
    ppermute x16 -> x0, starting transfers between devices: 88.1 us -> none  [the longest x8 74 us: padded(): before = lax.ppermute(last, axis, up)]
    pallas_call x0 -> x1, Pallas kernels: none -> 75.4 us  [local(): pl.pallas_call(functools.partial(kernel, wide, narrow), out_shape=(tile,...]
    ppermute x16 -> x0, waiting for transfers between devices: 39.1 us -> none  [the longest x8 26.3 us: padded(): after = lax.ppermute(initial, axis, down)]
    dynamic_update_slice x4 -> x0, local copies, waits for them, and re-layouts: 25.1 us -> none  [visit(): lax.dynamic_update_slice(running, region + contribution[0], (0, row_start...]
    dot_general x8 -> x0, matrix products: 22.4 us -> none  [right_apply(): jnp.einsum('nqac,qpcd->npad', values, table, preferred_element_type=jnp.f...]
    another operation x21 -> x0, other arithmetic: 20.4 us -> none
    another operation x2 -> x0, loops' own time: 14.3 us -> none  [apply_operator(): lax.fori_loop(0, counts[0, 0], visit, (total, jnp.float32(0.0)))]
  transfers between devices with their start and end apart: 16 -> 0, of which waited for: 11 -> 0; matrix products, arithmetic and copies ran while one was open for 5% -> 0% of each run, Pallas kernels for 0% -> 0%
where the time goes in v1:
time: 82 us; the launch traced here: 81.8 us
  Pallas kernels  75.4 us (92%)
  local copies, waits for them, and re-layouts  5.07 us (6%)
  between operations  1.29 us (2%)
    pallas_call x1, Pallas kernels, local(): pl.pallas_call(functools.partial(kernel, wide, narrow), out_shape=(tile,...  75.4 us
    unnamed x3, local copies, waits for them, and re-layouts  5.07 us

profile of v1, /device:TPU:1, one launch (start us, length us, event | category | flops | bytes accessed | tf_op | source)
XLA Modules:
  0.0 81.8 jit_solution(8713266929033060330)
XLA Ops:
  1.3 1.3 %copy.8.offs = s32[1,1,3,2]{3,2,1,0:T(4,128)} copy(s32[1,1,3,2]{2,3,1,0:T(2,128)} %param.9) | data formatting | bytes 48 | tf_op args[3]
  2.6 75.4 %shard_map.77 = (f32[2,256,256]{2,1,0:T(8,128)}, f32[2,256,256]{2,1,0:T(8,128)}) custom-call(s32[1,1,3,2]{3,2,1,0:T(4,128)} %copy.8.offs, s32[1,1]{1,0:T(1,128)S(6)} %copy.11.counts, bf16[2,512,512]{2,1,0:T(8,128)(2,1)} %constant.2.clone.tab_hbm, f32[2,256,256]{2,1,0:T(8,128)} %grad_hbm.1, bf16[4,2,256,256]{3,2,1,0:T(8,128)(2,1)} %probe_hbm.1, ...), custom_call_target="tpu_custom_call" | custom-call | tf_op jit(solution)/shard_map/pallas_call | solution.py:433
  78.1 1.9 %copy.12 = f32[2,256,256]{2,1,0:T(8,128)} copy(f32[2,256,256]{2,1,0:T(8,128)} %get-tuple-element.4) | data formatting | bytes 1048576
  79.9 1.9 %copy.13 = f32[2,256,256]{2,1,0:T(8,128)} copy(f32[2,256,256]{2,1,0:T(8,128)} %get-tuple-element.5) | data formatting | bytes 1048576
